TPU v7x, 512 devices: a whole 4x4x16 slice. The times are simulated.
512 devices in a mesh: leaf: 8 (over x, core), row: 8 (over y, z_hi), col: 8 (over z_lo).
Axes of the slice: x: 4, y: 4, z: 16 (z_hi: 2, z_lo: 8; z = z_hi * 8 + z_lo), core: 2. Of those that a mesh axis runs over, the one named last changes fastest.
Arguments:
- child_front: float32 [8, 4096, 4096], P('leaf', 'row', 'col'), as said below
- parent_front: bfloat16 [8192, 32768], P('row', ('leaf', 'col')), as said below
- block_map: int32 [8, 30], replicated, may hold values from 0 to 63, as said below
Outputs:
- child_panel_t: float32 [8, 256, 4096], P('leaf', 'col', 'row')
- parent_panel_t: float32 [1024, 8192], P(('leaf', 'col'), 'row')
- parent_update: float32 [8192, 32768], P('row', ('leaf', 'col'))
Inputs may be any that keep to these rules, and one draw needn't show every extreme that they name: `child_front`: every child front is symmetric positive definite. `parent_front`: every parent front (each block of 8192 columns) is symmetric positive definite. `block_map`: in each row the entries are distinct. Of the contribution blocks that one device of a child's grid holds in its rows, at most 1 go to parent blocks whose rows one index of row holds; of those it holds in its columns, at most 1 go to parent blocks whose columns are held by one index of col, counting both leaves of the pair together; of all contribution blocks of one child, at most 4 go to parent blocks whose rows one index of row holds. All three bounds are reached.
All inputs are finite; a program needn't handle non-finite values.
Results may differ from a plain program's by a relative error of at most 0.0003.
Values sent between devices are 32-bit elements; how exact they have to be, the bound alone decides.
No kernel may reach another device: no remote copies, remote signals or barrier semaphores. Data moves between devices by JAX's collectives and lax.ppermute only.
A program may use at most 64 MiB of HBM per device.

v0:
```python
import jax
import jax.numpy as jnp
from jax import lax
from jax.sharding import PartitionSpec as P

BLK = 128


def from_partner(value, axis, bit):
    mask = 2**bit
    pairs = [(source, source ^ mask) for source in range(lax.axis_size(axis))]
    return lax.ppermute(value, axis, pairs)


def from_root(value, axis, source):
    kept = jnp.where(lax.axis_index(axis) == source, value, 0).astype(value.dtype)
    return lax.psum(kept, axis)


def pair_swap(values):
    return from_partner(values, "leaf", 0)


def one_hot(values, size):
    return (values[:, None] == jnp.arange(size)[None, :]).astype(jnp.float32)


def factor_panel(front_block, panel_width, row_start, col_start, paired):
    precise_setting = lax.Precision.HIGHEST
    panel_slab = from_root(front_block[:, :panel_width], "col", 0)
    if paired:
        partner = pair_swap(panel_slab)
        panel_slab = jnp.where(lax.axis_index("leaf") % 2 == 0, panel_slab, partner)
    block_cols = front_block.shape[1]
    joined = jnp.concatenate((front_block[:panel_width], panel_slab[:panel_width]), axis=1)
    joined = from_root(joined, "row", 0)
    top_block = joined[:, :block_cols]
    diagonal_block = joined[:, block_cols:]
    lower_factor = jnp.linalg.cholesky(diagonal_block)
    identity = jnp.eye(panel_width, dtype=jnp.float32)
    inverse_factor = jax.scipy.linalg.solve_triangular(lower_factor, identity, lower=True)
    rows_factor = jnp.dot(panel_slab, inverse_factor.T, precision=precise_setting)
    cols_factor = jnp.dot(inverse_factor, top_block, precision=precise_setting)
    update = jnp.dot(rows_factor, cols_factor, precision=precise_setting)
    row_ids = row_start + jnp.arange(front_block.shape[0])
    col_ids = col_start + jnp.arange(block_cols)
    keep_mask = (row_ids[:, None] >= panel_width) & (col_ids[None, :] >= panel_width)
    schur_part = jnp.where(keep_mask, front_block - update, jnp.float32(0.0))
    return (rows_factor, schur_part)


def shards(child_front, parent_front, block_map):
    leaf_id = lax.axis_index("leaf")
    row_id = lax.axis_index("row")
    col_id = lax.axis_index("col")
    row_count = lax.axis_size("row")
    col_count = lax.axis_size("col")
    precise_setting = lax.Precision.HIGHEST
    child_block = child_front[0]
    child_rows, child_cols = child_block.shape
    panel_width = child_cols // 2
    rows_factor, contribution = factor_panel(
        child_block, panel_width, row_id * child_rows, col_id * child_cols, False
    )
    out_width = panel_width // col_count
    child_out = lax.dynamic_slice_in_dim(rows_factor, col_id * out_width, out_width, 1).T[None]
    parent_rows, parent_cols = parent_front.shape
    parent_order = parent_rows * row_count
    row_span = parent_rows // BLK
    col_span = parent_cols // BLK
    row_blocks = child_rows // BLK
    col_blocks = child_cols // BLK
    cap_rows = max(1, row_blocks // row_count)
    cap_cols = max(1, col_blocks // col_count)
    own_map = lax.dynamic_index_in_dim(block_map, leaf_id, 0, keepdims=False)
    block_count = own_map.shape[0]
    block_ids = jnp.arange(block_count)
    global_ids = panel_width + block_ids * BLK
    src_row = global_ids // child_rows
    src_col = global_ids // child_cols
    dst_row = own_map // row_span
    owner_col = own_map // col_span
    dst_col = owner_col % col_count
    dst_half = owner_col // col_count
    earlier = block_ids[None, :] < block_ids[:, None]
    rank_row = jnp.sum(
        earlier & (src_row[None, :] == src_row[:, None]) & (dst_row[None, :] == dst_row[:, None]),
        axis=1,
    )
    rank_col = jnp.sum(
        earlier & (src_col[None, :] == src_col[:, None]) & (dst_col[None, :] == dst_col[:, None]),
        axis=1,
    )
    local_rows = (global_ids - row_id * child_rows) // BLK
    local_cols = (global_ids - col_id * child_cols) // BLK
    row_pick = jnp.einsum(
        "k,kd,ka,kx->dax",
        (src_row == row_id).astype(jnp.float32),
        one_hot(dst_row, row_count),
        one_hot(rank_row, cap_rows),
        one_hot(local_rows, row_blocks),
        precision=precise_setting,
    )
    col_pick = jnp.einsum(
        "k,ke,kj,ky->ejy",
        (src_col == col_id).astype(jnp.float32),
        one_hot(dst_col, col_count),
        one_hot(rank_col, cap_cols),
        one_hot(local_cols, col_blocks),
        precision=precise_setting,
    )
    place_cols = jnp.einsum(
        "k,kh,ky,kc,kj->hycj",
        (dst_col == col_id).astype(jnp.float32),
        one_hot(dst_half, 2),
        one_hot(own_map % col_span, col_span),
        one_hot(src_col, col_count),
        one_hot(rank_col, cap_cols),
        precision=precise_setting,
    )
    strip_view = contribution.reshape(row_blocks, BLK, child_cols)
    strips = jnp.einsum("dax,xiw->daiw", row_pick, strip_view, precision=precise_setting)
    received_blocks = lax.all_to_all(
        strips.reshape(row_count, cap_rows * BLK, child_cols),
        "row",
        split_axis=0,
        concat_axis=0,
        tiled=True,
    )
    received_blocks = received_blocks.reshape(row_count, cap_rows, BLK, child_cols)
    on_this_row = (dst_row == row_id).astype(jnp.float32)
    rank_dest = jnp.sum(earlier & (dst_row[None, :] == dst_row[:, None]), axis=1)
    cap_incoming = -(-block_count // row_count)
    dense_selection = jnp.einsum(
        "c,cn,cw,cp->nwp",
        on_this_row,
        one_hot(rank_dest, cap_incoming),
        one_hot(src_row, row_count),
        one_hot(rank_row, cap_rows),
        precision=precise_setting,
    )
    squeezed_result = jnp.einsum(
        "byx,yxhq->bhq", dense_selection, received_blocks, precision=precise_setting
    )
    squeezed_result = squeezed_result.reshape(cap_incoming, BLK, col_blocks, BLK)
    sending = jnp.einsum("miyb,ejy->emijb", squeezed_result, col_pick, precision=precise_setting)
    landed = lax.all_to_all(
        sending.reshape(col_count, cap_incoming * BLK, cap_cols * BLK),
        "col",
        split_axis=0,
        concat_axis=0,
        tiled=True,
    )
    landed = landed.reshape(col_count, cap_incoming, BLK, cap_cols, BLK)
    place_rows = jnp.einsum(
        "k,kx,km->xm",
        on_this_row,
        one_hot(own_map % row_span, row_span),
        one_hot(rank_dest, cap_incoming),
        precision=precise_setting,
    )
    placed_rows = jnp.einsum("xm,cmijb->xcijb", place_rows, landed, precision=precise_setting)
    halves = jnp.einsum(
        "xcijb,hycj->hxiyb", placed_rows, place_cols, precision=precise_setting
    ).reshape(2, parent_rows, parent_cols)
    own_half = leaf_id % 2
    own_part = lax.dynamic_index_in_dim(halves, own_half, 0, keepdims=False)
    other_part = lax.dynamic_index_in_dim(halves, 1 - own_half, 0, keepdims=False)
    assembled = parent_front.astype(jnp.float32) + own_part + pair_swap(other_part)
    parent_width = parent_cols // 2
    col_start = own_half * (parent_order // 2) + col_id * parent_cols
    parent_factor, parent_schur = factor_panel(
        assembled, parent_width, row_id * parent_rows, col_start, True
    )
    share_width = parent_width // (2 * col_count)
    share_start = (own_half * col_count + col_id) * share_width
    parent_out = lax.dynamic_slice_in_dim(parent_factor, share_start, share_width, 1).T
    return (child_out, parent_out, parent_schur)


def solution(mesh):
    placed = (P("leaf", "row", "col"), P("row", ("leaf", "col")), P())
    return jax.shard_map(
        shards,
        mesh=mesh,
        in_specs=placed,
        out_specs=(P("leaf", "col", "row"), P(("leaf", "col"), "row"), P("row", ("leaf", "col"))),
        check_vma=False,
    )
```

profile of v0, /device:TPU:6, one launch (start us, length us, event | category | flops | bytes accessed | tf_op | source)
XLA Modules:
  0.0 1079.2 jit_solution(1554957028383324433)
XLA Ops:
  7.2 1.6 copy.64
  10.5 128.7 %all-reduce.6.cloned.1.call-done = f32[512,256]{0,1:T(8,128)} async-done(((f32[512,256]{0,1:T(8,128)}), f32[512,256]{0,1:T(8,128)}) %all-reduce.6.cloned.1.call-update) | async-done | bytes 524304 | tf_op jit(solution)/shard_map/psum | solution.py:17
  141.8 207.1 %all-reduce.8.cloned.1.call-done = f32[256,768]{0,1:T(8,128)} async-done(((f32[256,768]{0,1:T(8,128)}), f32[256,768]{0,1:T(8,128)}) %all-reduce.8.cloned.1.call-update) | async-done | bytes 786448 | tf_op jit(solution)/shard_map/psum | solution.py:17
  349.9 1.0 fusion.23
  350.9 11.7 %cholesky.130 = f32[128,128]{1,0:T(8,128)S(1)} custom-call(f32[128,128]{1,0:T(8,128)S(1)} %cholesky.194), custom_call_target="Cholesky" | custom-call | tf_op jit(solution)/shard_map/jit(cholesky)/cholesky | solution.py:39
  362.7 9.8 custom-call.13
  373.0 11.7 %cholesky.147 = f32[128,128]{1,0:T(8,128)S(1)} custom-call(f32[128,128]{1,0:T(8,128)S(1)} %convolution_subtract_fusion.4), custom_call_target="Cholesky" | custom-call | tf_op jit(solution)/shard_map/jit(cholesky)/cholesky | solution.py:39
  386.8 4.2 while.4
  387.6 1.4 bitcast_dynamic-update-slice_fusion.4
  389.6 1.4 bitcast_dynamic-update-slice_fusion.4
  391.0 19.7 %custom-call.14 = f32[2,128,128]{1,2,0:T(8,128)S(1)} custom-call(f32[2,128,128]{2,1,0:T(8,128)S(1)} %get-tuple-element.19), custom_call_target="InvertDiagBlocksLowerTriangular" | custom-call | tf_op jit(solution)/shard_map/jit(_solve_triangular)/triangular_solve | solution.py:41
  413.1 1.2 fusion.15
  415.2 2.3 fusion.82
  417.5 2.5 copy.70
  420.0 8.9 all-to-all-start
  429.5 79.5 %all-to-all-done = f32[8,128,512]{2,1,0:T(8,128)S(1)} async-done(((f32[8,128,512]{2,1,0:T(8,128)}), f32[8,128,512]{2,1,0:T(8,128)S(1)}, u32[]{:S(2)}, u32[]{:S(2)}) %all-to-all-start) | async-done | bytes 2097184 | tf_op jit(solution)/shard_map/all_to_all | solution.py:123
  509.0 2.8 fusion.12
  512.1 2.8 fusion.16
  515.0 1.7 copy.74
  516.7 13.0 %all-to-all-start.1 = ((f32[8,512,128]{2,1,0:T(8,128)}), f32[8,512,128]{2,1,0:T(8,128)S(1)}, u32[]{:S(2)}, u32[]{:S(2)}) async-start(f32[8,512,128]{2,1,0:T(8,128)} %copy.74), calls=%async_computation.1 | async-start | bytes 4194304 | tf_op jit(solution)/shard_map/all_to_all | solution.py:147
  530.4 95.4 %all-to-all-done.1 = f32[8,512,128]{2,1,0:T(8,128)S(1)} async-done(((f32[8,512,128]{2,1,0:T(8,128)}), f32[8,512,128]{2,1,0:T(8,128)S(1)}, u32[]{:S(2)}, u32[]{:S(2)}) %all-to-all-start.1) | async-done | bytes 2097184 | tf_op jit(solution)/shard_map/all_to_all | solution.py:147
  625.7 5.9 fusion.9
  631.7 8.4 fusion.3
  640.0 5.5 reshape.323
  645.5 4.0 constant_dynamic-slice_fusion.3
  649.5 2.9 copy.88
  652.4 2.1 collective-permute-start
  654.6 1.5 copy.67
  656.1 1.8 copy.87
  658.8 2.8 fusion.8
  661.6 1.2 slice_select_fusion
  662.9 127.0 %all-reduce.10.cloned.1.call-done = f32[1024,256]{0,1:T(8,128)} async-done(((f32[1024,256]{0,1:T(8,128)}), f32[1024,256]{0,1:T(8,128)}) %all-reduce.10.cloned.1.call-update) | async-done | bytes 1048592 | tf_op jit(solution)/shard_map/psum | solution.py:17
  789.9 1.9 collective-permute-start.1
  791.8 2.8 collective-permute-done.1
  794.6 1.4 broadcast_select_fusion
  797.1 1.5 dynamic-slice_bitcast_fusion.1
  798.6 204.2 %all-reduce.12.cloned.1.call-done = f32[256,768]{0,1:T(8,128)} async-done(((f32[256,768]{0,1:T(8,128)}), f32[256,768]{0,1:T(8,128)}) %all-reduce.12.cloned.1.call-update) | async-done | bytes 786448 | tf_op jit(solution)/shard_map/psum | solution.py:17
  1003.9 1.0 fusion.22
  1004.9 11.7 %cholesky.164 = f32[128,128]{1,0:T(8,128)S(1)} custom-call(f32[128,128]{1,0:T(8,128)S(1)} %cholesky.197), custom_call_target="Cholesky" | custom-call | tf_op jit(solution)/shard_map/jit(cholesky)/cholesky | solution.py:39
  1016.7 9.8 custom-call.15
  1027.0 11.7 %cholesky.181 = f32[128,128]{1,0:T(8,128)S(1)} custom-call(f32[128,128]{1,0:T(8,128)S(1)} %convolution_subtract_fusion.3), custom_call_target="Cholesky" | custom-call | tf_op jit(solution)/shard_map/jit(cholesky)/cholesky | solution.py:39
  1041.2 4.0 while.5
  1042.1 1.3 bitcast_dynamic-update-slice_fusion.5
  1043.9 1.3 bitcast_dynamic-update-slice_fusion.5
  1045.2 19.7 %custom-call.16 = f32[2,128,128]{1,2,0:T(8,128)S(1)} custom-call(f32[2,128,128]{2,1,0:T(8,128)S(1)} %get-tuple-element.20), custom_call_target="InvertDiagBlocksLowerTriangular" | custom-call | tf_op jit(solution)/shard_map/jit(_solve_triangular)/triangular_solve | solution.py:41
  1065.8 1.1 fusion.25
  1068.2 2.2 subtract_select_fusion
  1070.4 1.8 copy.81
  (95 shorter events, 20.9 us)
Async XLA Ops:
  7.2 132.1 %all-reduce.6.cloned.1.call-start = ((), (), s32[]{:S(2)}) async-start(), calls=%async_computation.2 | async-start | bytes 1048576 | tf_op jit(solution)/shard_map/psum | solution.py:17
  9.6 339.2 %all-reduce.8.cloned.1.call-start = ((), (), s32[]{:S(2)}) async-start(), calls=%async_computation.3 | async-start | bytes 1572864 | tf_op jit(solution)/shard_map/psum | solution.py:17
  350.9 60.7 %copy-start.5 = (f32[512,256]{0,1:T(8,128)S(1)}, f32[512,256]{0,1:T(8,128)}, u32[]{:S(2)}) copy-start(f32[512,256]{0,1:T(8,128)} %all-reduce.6.cloned.1.call-done) | copy-start | bytes 1572868
  373.0 39.2 %copy-start.4 = (f32[256,768]{0,1:T(8,128)S(1)}, f32[256,768]{0,1:T(8,128)}, u32[]{:S(2)}) copy-start(f32[256,768]{0,1:T(8,128)} %all-reduce.8.cloned.1.call-done) | copy-start | bytes 2359300
  412.2 0.8 copy-start.2
  420.0 88.9 %all-to-all-start = ((f32[8,128,512]{2,1,0:T(8,128)}), f32[8,128,512]{2,1,0:T(8,128)S(1)}, u32[]{:S(2)}, u32[]{:S(2)}) async-start(f32[8,128,512]{2,1,0:T(8,128)} %copy.70), calls=%async_computation | async-start | bytes 4194304 | tf_op jit(solution)/shard_map/all_to_all | solution.py:123
  516.7 109.0 %all-to-all-start.1 = ((f32[8,512,128]{2,1,0:T(8,128)}), f32[8,512,128]{2,1,0:T(8,128)S(1)}, u32[]{:S(2)}, u32[]{:S(2)}) async-start(f32[8,512,128]{2,1,0:T(8,128)} %copy.74), calls=%async_computation.1 | async-start | bytes 4194304 | tf_op jit(solution)/shard_map/all_to_all | solution.py:147
  529.7 260.1 %all-reduce.10.cloned.1.call-start = ((), (), s32[]{:S(2)}) async-start(), calls=%async_computation.4 | async-start | bytes 2097152 | tf_op jit(solution)/shard_map/psum | solution.py:17
  652.4 6.4 collective-permute-start
  661.6 130.2 %copy-start = (f32[1024,512]{0,1:T(8,128)}, f32[1024,512]{0,1:T(8,128)S(1)}, u32[]{:S(2)}) copy-start(f32[1024,512]{0,1:T(8,128)S(1)} %fusion.8) | copy-start | bytes 6291460
  662.8 340.0 %all-reduce.12.cloned.1.call-start = ((), (), s32[]{:S(2)}) async-start(), calls=%async_computation.5 | async-start | bytes 1572864 | tf_op jit(solution)/shard_map/psum | solution.py:17
  789.9 4.8 collective-permute-start.1
  794.6 1.5 slice-start
  1041.2 26.3 %copy-start.3 = (f32[256,768]{0,1:T(8,128)S(1)}, f32[256,768]{0,1:T(8,128)}, u32[]{:S(2)}) copy-start(f32[256,768]{0,1:T(8,128)} %all-reduce.12.cloned.1.call-done) | copy-start | bytes 2359300
  1065.5 2.7 copy-start.1
Sparse Core Ops, SparseCore 0:
  11.5 127.7 all-reduce.5
  143.1 205.7 all-reduce.7
  662.9 126.8 all-reduce.9
  797.2 205.5 all-reduce.11
where the time goes:
time: 1090 us; the launch traced here: 1080 us
  waiting for transfers between devices  846 us (78%)
  other arithmetic  119 us (11%)
  local copies, waits for them, and re-layouts  37.9 us (3%)
  matrix products  32.4 us (3%)
  starting transfers between devices  26.2 us (2%)
  between operations  17.3 us (2%)
    psum x4, waiting for transfers between devices, from_root(): return lax.psum(kept, axis)  667 us
    all_to_all x1, waiting for transfers between devices, shards(): lax.all_to_all(sending.reshape(col_count, cap_incoming * BLK, cap_cols *...  95.4 us
    all_to_all x1, waiting for transfers between devices, shards(): lax.all_to_all(strips.reshape(row_count, cap_rows * BLK, child_cols), 'ro...  79.5 us
    another operation x13, other arithmetic, factor_panel(): lower_factor = jnp.linalg.cholesky(diagonal_block)  68.5 us
    another operation x5, other arithmetic, factor_panel(): jax.scipy.linalg.solve_triangular(lower_factor, identity, lower=True)  39.4 us
  transfers between devices with their start and end apart: 8, of which 8 were waited for; matrix products, arithmetic and copies ran while one was open for 1% of the time, Pallas kernels for 0%

commit v1 on v0

--- a/solution.py
+++ b/solution.py
@@ -14,7 +14,7 @@
 
 def from_root(value, axis, source):
     kept = jnp.where(lax.axis_index(axis) == source, value, 0).astype(value.dtype)
-    return lax.psum(kept, axis)
+    return jnp.sum(lax.all_gather(kept, axis), 0)
 
 
 def pair_swap(values):

time: 1090 us -> 1190 us (1.092)
  the two profiles are of different devices: /device:TPU:6 before, /device:TPU:98 now
where the time goes in v1:
time: 1190 us; the launch traced here: 1180 us
  waiting for transfers between devices  941 us (79%)
  other arithmetic  136 us (11%)
  matrix products  37.4 us (3%)
  local copies, waits for them, and re-layouts  30.8 us (3%)
  between operations  17.4 us (1%)
  starting transfers between devices  13.7 us (1%)
    all_gather x4, waiting for transfers between devices, from_root(): return jnp.sum(lax.all_gather(kept, axis), 0)  761 us
    all_to_all x1, waiting for transfers between devices, shards(): lax.all_to_all(sending.reshape(col_count, cap_incoming * BLK, cap_cols *...  89.2 us
    all_to_all x1, waiting for transfers between devices, shards(): lax.all_to_all(strips.reshape(row_count, cap_rows * BLK, child_cols), 'ro...  83.6 us
    another operation x13, other arithmetic, factor_panel(): lower_factor = jnp.linalg.cholesky(diagonal_block)  69.3 us
    another operation x5, other arithmetic, factor_panel(): jax.scipy.linalg.solve_triangular(lower_factor, identity, lower=True)  41.9 us
  transfers between devices with their start and end apart: 8, of which 8 were waited for; matrix products, arithmetic and copies ran while one was open for 0% of the time, Pallas kernels for 0%

profile of v1, /device:TPU:98, one launch (start us, length us, event | category | flops | bytes accessed | tf_op | source)
XLA Modules:
  0.0 1176.8 jit_solution(3930161530986891701)
XLA Ops:
  7.2 1.9 slice_select_fusion.1
  10.3 99.7 %all-gather.11.cloned.1.call-done = f32[4096,256]{1,0:T(8,128)} async-done(((f32[512,256]{1,0:T(8,128)}), f32[4096,256]{1,0:T(8,128)}) %all-gather.11.cloned.1.call-update) | async-done | bytes 4194320 | tf_op jit(solution)/shard_map/all_gather | solution.py:17
  109.9 2.5 reduce_sum.63
  114.8 240.3 %all-gather.7.cloned.1.call-done = f32[8,256,768]{2,1,0:T(8,128)} async-done(((f32[1,256,768]{2,1,0:T(8,128)}), f32[8,256,768]{2,1,0:T(8,128)}) %all-gather.7.cloned.1.call-update) | async-done | bytes 6291472 | tf_op jit(solution)/shard_map/all_gather | solution.py:17
  355.1 3.2 reduce_sum.64
  358.6 11.7 cholesky.130
  370.4 9.8 custom-call.13
  380.7 11.7 cholesky.147
  394.6 4.5 while.4
  395.6 1.4 bitcast_dynamic-update-slice_fusion.4
  397.6 1.4 bitcast_dynamic-update-slice_fusion.4
  399.1 19.7 %custom-call.14 = f32[2,128,128]{1,2,0:T(8,128)S(1)} custom-call(f32[2,128,128]{2,1,0:T(8,128)S(1)} %get-tuple-element.19), custom_call_target="InvertDiagBlocksLowerTriangular" | custom-call | tf_op jit(solution)/shard_map/jit(_solve_triangular)/triangular_solve | solution.py:41
  422.1 2.8 fusion.18
  424.9 2.5 copy.39
  427.4 3.6 all-to-all-start
  431.6 83.6 %all-to-all-done = f32[8,128,512]{2,1,0:T(8,128)S(1)} async-done(((f32[8,128,512]{2,1,0:T(8,128)}), f32[8,128,512]{2,1,0:T(8,128)S(1)}, u32[]{:S(2)}, u32[]{:S(2)}) %all-to-all-start) | async-done | bytes 2097184 | tf_op jit(solution)/shard_map/all_to_all | solution.py:123
  515.2 2.8 fusion.12
  518.4 2.8 fusion.16
  521.2 1.7 copy.43
  522.9 5.8 all-to-all-start.1
  529.3 89.2 %all-to-all-done.1 = f32[8,512,128]{2,1,0:T(8,128)S(1)} async-done(((f32[8,512,128]{2,1,0:T(8,128)}), f32[8,512,128]{2,1,0:T(8,128)S(1)}, u32[]{:S(2)}, u32[]{:S(2)}) %all-to-all-start.1) | async-done | bytes 2097184 | tf_op jit(solution)/shard_map/all_to_all | solution.py:147
  618.4 5.9 fusion.9
  624.4 8.4 fusion.3
  632.8 5.5 reshape.379
  638.2 1.9 dynamic-slice_bitcast_fusion
  640.1 1.9 collective-permute-start
  642.0 4.2 collective-permute-done
  646.3 2.8 fusion.8
  650.2 180.8 %all-gather.13.cloned.1.call-done = f32[8192,256]{1,0:T(8,128)} async-done(((f32[1024,256]{1,0:T(8,128)}), f32[8192,256]{1,0:T(8,128)}) %all-gather.13.cloned.1.call-update) | async-done | bytes 8388624 | tf_op jit(solution)/shard_map/all_gather | solution.py:17
  831.0 4.1 reduce_sum.68
  835.1 2.1 collective-permute-start.1
  837.3 2.5 collective-permute-done.1
  839.8 1.4 broadcast_select_fusion
  842.2 1.5 dynamic-slice_bitcast_fusion.2
  843.7 240.2 %all-gather.9.cloned.1.call-done = f32[8,256,768]{2,1,0:T(8,128)} async-done(((f32[1,256,768]{2,1,0:T(8,128)}), f32[8,256,768]{2,1,0:T(8,128)}) %all-gather.9.cloned.1.call-update) | async-done | bytes 6291472 | tf_op jit(solution)/shard_map/all_gather | solution.py:17
  1083.9 4.1 reduce_sum.69
  1088.0 1.7 slice.94
  1089.7 1.8 copy.52
  1093.2 11.7 cholesky.164
  1105.7 9.8 custom-call.15
  1115.5 1.7 constant_dynamic-update-slice_fusion
  1118.3 11.7 cholesky.181
  1133.2 1.7 select_select_fusion
  1134.9 6.1 while.5
  1135.8 2.3 bitcast_dynamic-update-slice_fusion.5
  1138.8 2.2 bitcast_dynamic-update-slice_fusion.5
  1141.6 20.5 %custom-call.16 = f32[2,128,128]{1,2,0:T(8,128)S(1)} custom-call(f32[2,128,128]{2,1,0:T(8,128)} %copy-done.6), custom_call_target="InvertDiagBlocksLowerTriangular" | custom-call | tf_op jit(solution)/shard_map/jit(_solve_triangular)/triangular_solve | solution.py:41
  1166.2 3.6 subtract_select_fusion
  (94 shorter events, 24.8 us)
Async XLA Ops:
  7.2 102.8 %all-gather.11.cloned.1.call-start = ((), (), s32[]{:S(2)}) async-start(), calls=%async_computation.4 | async-start | bytes 4718592 | tf_op jit(solution)/shard_map/all_gather | solution.py:17
  9.1 346.0 %all-gather.7.cloned.1.call-start = ((), (), s32[]{:S(2)}) async-start(), calls=%async_computation.2 | async-start | bytes 7077888 | tf_op jit(solution)/shard_map/all_gather | solution.py:17
  394.6 26.3 %copy-start.2 = (f32[1,512,512]{2,1,0:T(8,128)S(1)}, f32[1,512,512]{2,1,0:T(8,128)}, u32[]{:S(2)}) copy-start(f32[1,512,512]{2,1,0:T(8,128)} %param.6) | copy-start | bytes 3145732
  420.3 1.8 copy-start.3
  427.4 87.7 %all-to-all-start = ((f32[8,128,512]{2,1,0:T(8,128)}), f32[8,128,512]{2,1,0:T(8,128)S(1)}, u32[]{:S(2)}, u32[]{:S(2)}) async-start(f32[8,128,512]{2,1,0:T(8,128)} %copy.39), calls=%async_computation | async-start | bytes 4194304 | tf_op jit(solution)/shard_map/all_to_all | solution.py:123
  522.9 95.6 %all-to-all-start.1 = ((f32[8,512,128]{2,1,0:T(8,128)}), f32[8,512,128]{2,1,0:T(8,128)S(1)}, u32[]{:S(2)}, u32[]{:S(2)}) async-start(f32[8,512,128]{2,1,0:T(8,128)} %copy.43), calls=%async_computation.1 | async-start | bytes 4194304 | tf_op jit(solution)/shard_map/all_to_all | solution.py:147
  528.6 302.4 %all-gather.13.cloned.1.call-start = ((), (), s32[]{:S(2)}) async-start(), calls=%async_computation.5 | async-start | bytes 9437184 | tf_op jit(solution)/shard_map/all_gather | solution.py:17
  638.2 8.0 copy-start.4
  640.1 6.2 collective-permute-start
  650.2 433.7 %all-gather.9.cloned.1.call-start = ((), (), s32[]{:S(2)}) async-start(), calls=%async_computation.3 | async-start | bytes 7077888 | tf_op jit(solution)/shard_map/all_gather | solution.py:17
  835.1 2.2 copy-start.1
  835.1 4.7 collective-permute-start.1
  1092.5 0.7 copy-start.5
  1141.0 0.7 copy-start.6
  1162.1 2.8 copy-start
Sparse Core Ops, SparseCore 0:
  10.7 99.2 all-gather.10
  113.7 241.3 all-gather.6
  650.3 180.6 all-gather.12
  842.3 241.5 all-gather.8
